TPU v7x, 256 devices: a whole 4x4x8 slice. The times are simulated.
256 devices in a mesh: gx: 8 (over y, z_hi), gy: 8 (over x, core), gz: 4 (over z_lo).
Axes of the slice: x: 4, y: 4, z: 8 (z_hi: 2, z_lo: 4; z = z_hi * 4 + z_lo), core: 2. Of those that a mesh axis runs over, the one named last changes fastest.
Arguments:
- volume: bfloat16 [32, 64, 64, 128], P('gz', 'gx', 'gy'), may hold values from -6 to 6
- cotangent: bfloat16 [32, 64, 64, 128], P('gz', 'gx', 'gy'), may hold values from -0.0390625 to 0.0390625
- w_conv: bfloat16 [128, 27, 128], replicated, may hold values from -0.109375 to 0.109375
- w_down: bfloat16 [8, 128, 512], replicated, may hold values from -0.25 to 0.25
- w_bottle: bfloat16 [512, 27, 512], P(None, None, 'gz'), may hold values from -0.0546875 to 0.0546875
- w_up: bfloat16 [8, 512, 128], replicated, may hold values from -0.375 to 0.375
Outputs:
- output: bfloat16 [32, 64, 64, 128], P('gz', 'gx', 'gy')
- grad_conv: float32 [128, 27, 128], P(('gx', 'gy'))
- grad_bottle: float32 [512, 27, 512], P(('gx', 'gy'), None, 'gz')
All inputs are finite; a program needn't handle non-finite values.
Results may differ from a plain program's by a relative error of at most 0.015.
Values may be sent and summed in bfloat16 or wider, within the bound.
A program may use at most 64 MiB of HBM per device.

v0:
```python
import jax
import jax.numpy as jnp
from jax import lax
from jax.sharding import PartitionSpec as P


def with_halo(cells, sides, width):
    for axis, dim in sides:
        count = lax.axis_size(axis)
        ends = count - 1
        head = lax.slice_in_dim(cells, 0, width, axis=dim)
        tail = lax.slice_in_dim(cells, cells.shape[dim] - width, cells.shape[dim], axis=dim)
        cells = jnp.concatenate(
            [
                lax.ppermute(tail, axis, [(i, (i + 1) % count) for i in range(ends)]),
                cells,
                lax.ppermute(head, axis, [((i + 1) % count, i) for i in range(ends)]),
            ],
            axis=dim,
        )
    return cells


def silu_slope(values):
    sig = jax.nn.sigmoid(values)
    return sig * (1.0 + values * (1.0 - sig))


def conv_forward(padded, weight, extent):
    size_z, size_x, size_y = extent
    count_cells = size_z * size_x * size_y
    summed = jnp.zeros((count_cells, weight.shape[2]), jnp.float32)
    for tap_index in range(27):
        shift_z, shift_x, shift_y = (tap_index // 9, tap_index // 3 % 3, tap_index % 3)
        window = padded[
            shift_z : shift_z + size_z, shift_x : shift_x + size_x, shift_y : shift_y + size_y, :
        ]
        window = window.reshape(count_cells, padded.shape[3])
        summed = summed + jnp.dot(
            window, weight[:, tap_index, :], preferred_element_type=jnp.float32
        )
    return summed.reshape(size_z, size_x, size_y, weight.shape[2])


def conv_weight_grad(padded, gradient, extent):
    size_z, size_x, size_y = extent
    count_cells = size_z * size_x * size_y
    flat_gradient = gradient.reshape(count_cells, gradient.shape[3])
    pieces = []
    for tap_index in range(27):
        shift_z, shift_x, shift_y = (tap_index // 9, tap_index // 3 % 3, tap_index % 3)
        window = padded[
            shift_z : shift_z + size_z, shift_x : shift_x + size_x, shift_y : shift_y + size_y, :
        ]
        window = window.reshape(count_cells, padded.shape[3])
        pieces.append(
            lax.dot_general(
                window, flat_gradient, (((0,), (0,)), ((), ())), preferred_element_type=jnp.float32
            )
        )
    return jnp.stack(pieces, axis=1)


def conv_input_grad(padded, weight, extent):
    size_z, size_x, size_y = extent
    count_cells = size_z * size_x * size_y
    summed = jnp.zeros((count_cells, weight.shape[0]), jnp.float32)
    for tap_index in range(27):
        shift_z, shift_x, shift_y = (2 - tap_index // 9, 2 - tap_index // 3 % 3, 2 - tap_index % 3)
        window = padded[
            shift_z : shift_z + size_z, shift_x : shift_x + size_x, shift_y : shift_y + size_y, :
        ]
        window = window.reshape(count_cells, padded.shape[3])
        summed = summed + lax.dot_general(
            window,
            weight[:, tap_index, :],
            (((1,), (1,)), ((), ())),
            preferred_element_type=jnp.float32,
        )
    return summed.reshape(size_z, size_x, size_y, weight.shape[0])


def pool_features(fine, kernel):
    size_z, size_x, size_y, channels = fine.shape
    blocks = fine.reshape(size_z // 2, 2, size_x // 2, 2, size_y // 2, 2, channels)
    kernel_cube = kernel.reshape(2, 2, 2, kernel.shape[1], kernel.shape[2])
    return jnp.einsum(
        "zaxbycf,abcfg->zxyg", blocks, kernel_cube, preferred_element_type=jnp.float32
    )


def pool_adjoint(coarse_in, kernel):
    size_z, size_x, size_y, wide_channels = coarse_in.shape
    kernel_cube = kernel.reshape(2, 2, 2, kernel.shape[1], kernel.shape[2])
    result = jnp.einsum(
        "zxyg,abcfg->zaxbycf", coarse_in, kernel_cube, preferred_element_type=jnp.float32
    )
    return result.reshape(2 * size_z, 2 * size_x, 2 * size_y, kernel.shape[1])


def lift_features(coarse_in, kernel):
    size_z, size_x, size_y, wide_channels = coarse_in.shape
    kernel_cube = kernel.reshape(2, 2, 2, kernel.shape[1], kernel.shape[2])
    result = jnp.einsum(
        "zxyg,abcgf->zaxbycf", coarse_in, kernel_cube, preferred_element_type=jnp.float32
    )
    return result.reshape(2 * size_z, 2 * size_x, 2 * size_y, kernel.shape[2])


def lift_adjoint(fine, kernel):
    size_z, size_x, size_y, channels = fine.shape
    blocks = fine.reshape(size_z // 2, 2, size_x // 2, 2, size_y // 2, 2, channels)
    kernel_cube = kernel.reshape(2, 2, 2, kernel.shape[1], kernel.shape[2])
    return jnp.einsum(
        "zaxbycf,abcgf->zxyg", blocks, kernel_cube, preferred_element_type=jnp.float32
    )


def body(volume, cotangent, w_conv, w_down, w_bottle, w_up):
    size_z, size_x, size_y, channels = volume.shape
    group_channels = w_bottle.shape[2]
    half_x = size_x // 2
    half_y = size_y // 2
    padded = with_halo(volume, (("gx", 1), ("gy", 2), ("gz", 0)), 1)
    pre_hidden = conv_forward(padded, w_conv, (size_z, size_x, size_y))
    hidden = jax.nn.silu(pre_hidden).astype(jnp.bfloat16)
    hidden_slope = silu_slope(pre_hidden)
    coarse = pool_features(hidden, w_down).astype(jnp.bfloat16)
    stacked = lax.all_gather(coarse, "gz", axis=0, tiled=True)
    rimmed = with_halo(stacked, (("gx", 1), ("gy", 2)), 1)
    column_z = rimmed.shape[0]
    coarse_pad = jnp.pad(rimmed, ((1, 1), (0, 0), (0, 0), (0, 0)))
    pre_bottle = conv_forward(coarse_pad, w_bottle, (column_z, half_x, half_y))
    bottle = jax.nn.silu(pre_bottle).astype(jnp.bfloat16)
    bottle_slope = silu_slope(pre_bottle)
    own_start = lax.axis_index("gz") * group_channels
    own_up = lax.dynamic_slice_in_dim(w_up, own_start, group_channels, 1)
    lifted = lax.psum_scatter(
        lift_features(bottle, own_up).astype(jnp.bfloat16), "gz", scatter_dimension=0, tiled=True
    ).astype(jnp.float32)
    output = (lifted + hidden.astype(jnp.float32)).astype(jnp.bfloat16)
    back_bottle = lift_adjoint(cotangent, w_up).astype(jnp.bfloat16)
    split_grad = lax.all_to_all(back_bottle, "gz", split_axis=3, concat_axis=0, tiled=True)
    bottle_grad = (split_grad.astype(jnp.float32) * bottle_slope).astype(jnp.bfloat16)
    grad_bottle = lax.psum_scatter(
        conv_weight_grad(coarse_pad, bottle_grad, (column_z, half_x, half_y)),
        ("gx", "gy"),
        scatter_dimension=0,
        tiled=True,
    )
    grad_rimmed = with_halo(bottle_grad, (("gx", 1), ("gy", 2)), 1)
    grad_pad = jnp.pad(grad_rimmed, ((1, 1), (0, 0), (0, 0), (0, 0)))
    coarse_grad = lax.psum_scatter(
        conv_input_grad(
            grad_pad, w_bottle, (lax.axis_size("gz") * (size_z // 2), half_x, half_y)
        ).astype(jnp.bfloat16),
        "gz",
        scatter_dimension=0,
        tiled=True,
    )
    hidden_grad = (
        (pool_adjoint(coarse_grad, w_down) + cotangent.astype(jnp.float32)) * hidden_slope
    ).astype(jnp.bfloat16)
    full_term = conv_weight_grad(padded, hidden_grad, (size_z, size_x, size_y))
    depth_summed = lax.psum(full_term.astype(jnp.bfloat16), "gz").astype(jnp.float32)
    grad_conv = lax.psum_scatter(depth_summed, ("gx", "gy"), scatter_dimension=0, tiled=True)
    return (output, grad_conv, grad_bottle)


def solution(mesh):
    in_specs = (
        P("gz", "gx", "gy", None),
        P("gz", "gx", "gy", None),
        P(),
        P(),
        P(None, None, "gz"),
        P(),
    )
    out_specs = (
        P("gz", "gx", "gy", None),
        P(("gx", "gy"), None, None),
        P(("gx", "gy"), None, "gz"),
    )
    return jax.shard_map(body, mesh=mesh, in_specs=in_specs, out_specs=out_specs, check_vma=False)
```

profile of v0, /device:TPU:0, one launch (start us, length us, event | category | flops | bytes accessed | tf_op | source)
XLA Modules:
  0.0 818.0 jit_solution(18367334462036747407)
XLA Ops:
  10.1 8.5 %collective-permute-start = (bf16[8,1,8,128]{3,2,1,0:T(8,128)(2,1)S(1)}, bf16[8,1,8,128]{3,2,1,0:T(8,128)(2,1)S(1)}, u32[]{:S(2)}, u32[]{:S(2)}) collective-permute-start(bf16[8,1,8,128]{3,2,1,0:T(8,128)(2,1)S(1)} %get-tuple-element.94), channel_id=1, source_target_pairs={{0,32},{32,64},{64,96},{96,128},{128,160},{160,192},{192,224},{1,3... | collective-permute-start | bytes 49160 | tf_op jit(solution)/shard_map/ppermute | solution.py:15
  20.0 1.9 copy.315
  21.9 4.8 reshape.498
  26.7 4.2 all-to-all-start
  35.9 2.6 collective-permute-done.3
  38.5 3.9 collective-permute-start.4
  45.4 3.1 collective-permute-done.5
  55.1 14.3 %all_gather.3 = bf16[16,4,4,512]{3,2,1,0:T(4,128)(2,1)S(1)} all-gather(bf16[4,4,4,512]{3,2,1,0:T(4,128)(2,1)S(1)} %fusion.33), channel_id=1, replica_groups=mesh['gx'=8,'gy'=8,'gz'=4] {'gz'}, dimensions={0}, use_global_device_ids=true | all-gather | bytes 327680 | tf_op jit(solution)/shard_map/all_gather | solution.py:129
  70.1 8.6 %collective-permute-start.6 = (bf16[16,1,4,512]{3,0,2,1:T(8,128)(2,1)}, bf16[16,1,4,512]{3,0,2,1:T(8,128)(2,1)}, u32[]{:S(2)}, u32[]{:S(2)}) collective-permute-start(bf16[16,1,4,512]{3,0,2,1:T(8,128)(2,1)} %copy.428), channel_id=1, source_target_pairs={{0,32},{32,64},{64,96},{96,128},{128,160},{160,192},{192,224},{1,3... | collective-permute-start | bytes 196616 | tf_op jit(solution)/shard_map/ppermute | solution.py:15
  82.1 5.3 reshape.499
  92.8 1.9 collective-permute-start.8
  96.0 2.7 convert_bitcast_fusion
  98.6 2.6 copy.316
  101.2 4.2 copy.332
  116.8 2.0 fusion.356
  125.1 1.9 copy.309
  128.7 1.9 copy.308
  187.7 6.8 collective-permute-start.10
  204.1 3.8 collective-permute-start.12
  209.3 4.1 collective-permute-done.13
  229.4 44.6 %all-reduce.10.cloned.1.call-done = bf16[16,4,4,512]{3,2,1,0:T(4,128)(2,1)} async-done(((bf16[16,4,4,512]{3,2,1,0:T(4,128)(2,1)}), bf16[16,4,4,512]{3,2,1,0:T(4,128)(2,1)}) %all-reduce.10.cloned.1.call-update) | async-done | bytes 262160
  275.4 26.7 %reduce-scatter.4.cloned.1.call-done = bf16[8,8,8,128]{3,2,1,0:T(8,128)(2,1)} async-done(((bf16[32,8,8,128]{3,2,1,0:T(8,128)(2,1)}), bf16[8,8,8,128]{3,2,1,0:T(8,128)(2,1)}) %reduce-scatter.4.cloned.1.call-update) | async-done | bytes 131088 | tf_op jit(solution)/shard_map/reduce_scatter | solution.py:138
  317.8 55.8 %all-reduce.8.cloned.1.call-done = bf16[128,27,128]{2,0,1:T(8,128)(2,1)} async-done(((bf16[128,27,128]{2,0,1:T(8,128)(2,1)}), bf16[128,27,128]{2,0,1:T(8,128)(2,1)}) %all-reduce.8.cloned.1.call-update) | async-done | bytes 884752 | tf_op jit(solution)/shard_map/psum | solution.py:165
  373.6 436.3 %all-reduce.11 = f32[128,27,128]{2,0,1:T(8,128)S(1)} all-reduce(bf16[128,27,128]{2,0,1:T(8,128)(2,1)} %all-reduce.8.cloned.1.call-done), channel_id=4, replica_groups=mesh['gx'=8,'gy'=8,'gz'=4] {'gx','gy'}, use_global_device_ids=true, to_apply=%region_3.4.clone | all-reduce | flops 442368 | bytes 2654208
  (418 shorter events, 146.5 us)
Async XLA Ops:
  8.8 23.4 %collective-permute-start.1 = (bf16[8,1,8,128]{3,2,1,0:T(8,128)(2,1)S(1)}, bf16[8,1,8,128]{3,2,1,0:T(8,128)(2,1)S(1)}, u32[]{:S(2)}, u32[]{:S(2)}) collective-permute-start(bf16[8,1,8,128]{3,2,1,0:T(8,128)(2,1)S(1)} %get-tuple-element.93), channel_id=1, source_target_pairs={{32,0},{64,32},{96,64},{128,96},{160,128},{192,160},{224,192},{33,... | collective-permute-start | bytes 49160 | tf_op jit(solution)/shard_map/ppermute | solution.py:17
  10.1 22.0 %collective-permute-start = (bf16[8,1,8,128]{3,2,1,0:T(8,128)(2,1)S(1)}, bf16[8,1,8,128]{3,2,1,0:T(8,128)(2,1)S(1)}, u32[]{:S(2)}, u32[]{:S(2)}) collective-permute-start(bf16[8,1,8,128]{3,2,1,0:T(8,128)(2,1)S(1)} %get-tuple-element.94), channel_id=1, source_target_pairs={{0,32},{32,64},{64,96},{96,128},{128,160},{160,192},{192,224},{1,3... | collective-permute-start | bytes 49160 | tf_op jit(solution)/shard_map/ppermute | solution.py:15
  26.7 55.4 %all-to-all-start = ((bf16[4,2,4096]{2,1,0:T(2,128)(2,1)}), bf16[4,2,4096]{2,1,0:T(2,128)(2,1)}, u32[]{:S(2)}, u32[]{:S(2)}) async-start(bf16[4,2,4096]{2,1,0:T(2,128)(2,1)} %reshape.498), calls=%async_computation.1 | async-start | bytes 131072 | tf_op jit(solution)/shard_map/all_to_all | solution.py:143
  30.9 243.1 %all-reduce.10.cloned.1.call-start = ((), (), s32[]{:S(2)}) async-start(), calls=%async_computation.6 | async-start | bytes 524288
  32.4 3.6 collective-permute-start.2
  33.7 4.8 collective-permute-start.3
  38.5 6.8 collective-permute-start.4
  42.5 6.0 collective-permute-start.5
  70.1 17.3 %collective-permute-start.6 = (bf16[16,1,4,512]{3,0,2,1:T(8,128)(2,1)}, bf16[16,1,4,512]{3,0,2,1:T(8,128)(2,1)}, u32[]{:S(2)}, u32[]{:S(2)}) collective-permute-start(bf16[16,1,4,512]{3,0,2,1:T(8,128)(2,1)} %copy.428), channel_id=1, source_target_pairs={{0,32},{32,64},{64,96},{96,128},{128,160},{160,192},{192,224},{1,3... | collective-permute-start | bytes 196616 | tf_op jit(solution)/shard_map/ppermute | solution.py:15
  80.8 10.4 %collective-permute-start.7 = (bf16[16,1,4,512]{3,0,2,1:T(8,128)(2,1)}, bf16[16,1,4,512]{3,0,2,1:T(8,128)(2,1)}, u32[]{:S(2)}, u32[]{:S(2)}) collective-permute-start(bf16[16,1,4,512]{3,0,2,1:T(8,128)(2,1)} %copy.429), channel_id=1, source_target_pairs={{32,0},{64,32},{96,64},{128,96},{160,128},{192,160},{224,192},{33,... | collective-permute-start | bytes 196616 | tf_op jit(solution)/shard_map/ppermute | solution.py:17
  92.8 15.7 %collective-permute-start.8 = (bf16[16,6,1,512]{3,0,2,1:T(8,128)(2,1)}, bf16[16,6,1,512]{3,0,2,1:T(8,128)(2,1)}, u32[]{:S(2)}, u32[]{:S(2)}) collective-permute-start(bf16[16,6,1,512]{3,0,2,1:T(8,128)(2,1)} %get-tuple-element.30), channel_id=1, source_target_pairs={{0,4},{4,8},{8,12},{12,16},{16,20},{20,24},{24,28},{1,5},{5,9},{9,... | collective-permute-start | bytes 294920 | tf_op jit(solution)/shard_map/ppermute | solution.py:15
  94.7 13.8 %collective-permute-start.9 = (bf16[16,6,1,512]{3,0,2,1:T(8,128)(2,1)}, bf16[16,6,1,512]{3,0,2,1:T(8,128)(2,1)S(1)}, u32[]{:S(2)}, u32[]{:S(2)}) collective-permute-start(bf16[16,6,1,512]{3,0,2,1:T(8,128)(2,1)} %get-tuple-element.31), channel_id=1, source_target_pairs={{4,0},{8,4},{12,8},{16,12},{20,16},{24,20},{28,24},{5,1},{9,5},{13... | collective-permute-start | bytes 294920 | tf_op jit(solution)/shard_map/ppermute | solution.py:17
  187.7 15.4 %collective-permute-start.10 = (bf16[16,1,4,128]{3,0,2,1:T(8,128)(2,1)S(1)}, bf16[16,1,4,128]{3,0,2,1:T(8,128)(2,1)S(1)}, u32[]{:S(2)}, u32[]{:S(2)}) collective-permute-start(bf16[16,1,4,128]{3,0,2,1:T(8,128)(2,1)S(1)} %get-tuple-element.107), channel_id=1, source_target_pairs={{0,32},{32,64},{64,96},{96,128},{128,160},{160,192},{192,224},{1,3... | collective-permute-start | bytes 49160 | tf_op jit(solution)/shard_map/ppermute | solution.py:15
  194.5 9.5 %collective-permute-start.11 = (bf16[16,1,4,128]{3,0,2,1:T(8,128)(2,1)S(1)}, bf16[16,1,4,128]{3,0,2,1:T(8,128)(2,1)S(1)}, u32[]{:S(2)}, u32[]{:S(2)}) collective-permute-start(bf16[16,1,4,128]{3,0,2,1:T(8,128)(2,1)S(1)} %get-tuple-element.108), channel_id=1, source_target_pairs={{32,0},{64,32},{96,64},{128,96},{160,128},{192,160},{224,192},{33,... | collective-permute-start | bytes 49160 | tf_op jit(solution)/shard_map/ppermute | solution.py:17
  204.1 5.2 collective-permute-start.12
  207.9 5.5 collective-permute-start.13
  221.8 80.3 %reduce-scatter.4.cloned.1.call-start = ((), (), s32[]{:S(2)}) async-start(), calls=%async_computation.3 | async-start | bytes 655360 | tf_op jit(solution)/shard_map/reduce_scatter | solution.py:138
  225.2 48.8 %copy-start.64 = (bf16[8,128,512]{2,1,0:T(8,128)(2,1)S(1)}, bf16[8,128,512]{2,1,0:T(8,128)(2,1)}, u32[]{:S(2)}) copy-start(bf16[8,128,512]{2,1,0:T(8,128)(2,1)} %param.9) | copy-start | bytes 3145732
  225.2 148.4 %all-reduce.8.cloned.1.call-start = ((), (), s32[]{:S(2)}) async-start(), calls=%async_computation.4 | async-start | bytes 1769472 | tf_op jit(solution)/shard_map/psum | solution.py:165
  227.4 74.7 %copy-start.59 = (f32[512,128]{1,0:T(8,128)S(1)}, f32[512,128]{1,0:T(8,128)}, u32[]{:S(2)}) copy-start(f32[512,128]{1,0:T(8,128)} %get-tuple-element.118) | copy-start | bytes 786436
  227.4 74.7 %copy-start.62 = (bf16[8,8,8,128]{3,2,1,0:T(8,128)(2,1)S(1)}, bf16[8,8,8,128]{3,2,1,0:T(8,128)(2,1)}, u32[]{:S(2)}) copy-start(bf16[8,8,8,128]{3,2,1,0:T(8,128)(2,1)} %param.7) | copy-start | bytes 393220
  227.5 76.4 %copy-start.5 = (bf16[9,10,10,128]{3,2,1,0:T(8,128)(2,1)S(1)}, bf16[9,10,10,128]{3,2,1,0:T(8,128)(2,1)}, u32[]{:S(2)}) copy-start(bf16[9,10,10,128]{3,2,1,0:T(8,128)(2,1)} %copy-done.4) | copy-start | bytes 691204
  311.7 498.9 %reduce-scatter.6.cloned.1.call-start = ((), (), s32[]{:S(2)}) async-start(), calls=%async_computation.5 | async-start | bytes 7188480 | tf_op jit(solution)/shard_map/reduce_scatter | solution.py:145
  315.8 494.8 %copy-start.1 = (bf16[8,512,128]{2,1,0:T(8,128)(2,1)S(1)}, bf16[8,512,128]{2,1,0:T(8,128)(2,1)}, u32[]{:S(2)}) copy-start(bf16[8,512,128]{2,1,0:T(8,128)(2,1)} %param.11) | copy-start | bytes 3145732
  (62 other events, 344.0 us)
Sparse Core Ops, SparseCore 0:
  221.9 52.0 all-reduce.9
  276.7 25.4 reduce-scatter.3
  311.8 61.7 all-reduce.7
Sparse Core Ops, SparseCore 1:
  315.9 434.7 reduce-scatter.5
where the time goes:
time: 828 us; the launch traced here: 818 us
  blocking collectives  451 us (54%)
  waiting for transfers between devices  140 us (17%)
  local copies, waits for them, and re-layouts  100 us (12%)
  matrix products  52 us (6%)
  starting transfers between devices  48.4 us (6%)
  between operations  19 us (2%)
    unnamed x1, blocking collectives  436 us
    psum x1, waiting for transfers between devices, body(): lax.psum(full_term.astype(jnp.bfloat16), 'gz').astype(jnp.float32)  55.8 us
    unnamed x5, waiting for transfers between devices  44.7 us
    reshape x27, local copies, waits for them, and re-layouts, conv_forward(): window = window.reshape(count_cells, padded.shape[3])  36.5 us
    ppermute x7, starting transfers between devices, with_halo(): lax.ppermute(tail, axis, [(i, (i + 1) % count) for i in range(ends)])  34.7 us
    slice x32, local copies, waits for them, and re-layouts, conv_forward(): padded[shift_z:shift_z + size_z, shift_x:shift_x + size_x, shift_y:shift_...  31.6 us
    reduce_scatter x1, waiting for transfers between devices, body(): lax.psum_scatter(lift_features(bottle, own_up).astype(jnp.bfloat16), 'gz'...  26.7 us
    dot_general x54, matrix products, conv_weight_grad(): lax.dot_general(window, flat_gradient, (((0,), (0,)), ((), ())), preferre...  23.6 us
  transfers between devices with their start and end apart: 19, of which 8 were waited for; matrix products, arithmetic and copies ran while one was open for 7% of the time, Pallas kernels for 0%

commit v1 on v0

--- a/solution.py
+++ b/solution.py
@@ -162,7 +162,9 @@
         (pool_adjoint(coarse_grad, w_down) + cotangent.astype(jnp.float32)) * hidden_slope
     ).astype(jnp.bfloat16)
     full_term = conv_weight_grad(padded, hidden_grad, (size_z, size_x, size_y))
-    depth_summed = lax.psum(full_term.astype(jnp.bfloat16), "gz").astype(jnp.float32)
+    depth_summed = jnp.sum(lax.all_gather(full_term.astype(jnp.bfloat16), "gz"), axis=0).astype(
+        jnp.float32
+    )
     grad_conv = lax.psum_scatter(depth_summed, ("gx", "gy"), scatter_dimension=0, tiled=True)
     return (output, grad_conv, grad_bottle)
 

time: 828 us -> 872 us (1.053)
  matrix products: 52 us -> 87.5 us
  local copies, waits for them, and re-layouts: 100 us -> 115 us
    psum x1 -> x0, waiting for transfers between devices: 55.8 us -> none  [body(): lax.psum(full_term.astype(jnp.bfloat16), 'gz').astype(jnp.float32)]
    all_gather x0 -> x1, waiting for transfers between devices: none -> 43.3 us  [body(): lax.all_gather(full_term.astype(jnp.bfloat16), 'gz')]
    dot_general x54, matrix products: 23.6 us -> 54.4 us  [conv_weight_grad(): lax.dot_general(window, flat_gradient, (((0,), (0,)), ((), ())), preferre...]
    ppermute x7, waiting for transfers between devices: 12.5 us -> 25.7 us  [with_halo(): lax.ppermute(head, axis, [((i + 1) % count, i) for i in range(ends)])]
    slice x32, local copies, waits for them, and re-layouts: 31.6 us -> 41.4 us  [conv_forward(): padded[shift_z:shift_z + size_z, shift_x:shift_x + size_x, shift_y:shift_...]
  transfers between devices with their start and end apart: 19 -> 19, of which waited for: 8 -> 10; matrix products, arithmetic and copies ran while one was open for 7% -> 9% of each run, Pallas kernels for 0% -> 0%
where the time goes in v1:
time: 872 us; the launch traced here: 860 us
  blocking collectives  443 us (51%)
  waiting for transfers between devices  141 us (16%)
  local copies, waits for them, and re-layouts  115 us (13%)
  matrix products  87.5 us (10%)
  starting transfers between devices  42.3 us (5%)
  between operations  18.6 us (2%)
  other arithmetic  12.3 us (1%)
    unnamed x1, blocking collectives  429 us
    dot_general x54, matrix products, conv_weight_grad(): lax.dot_general(window, flat_gradient, (((0,), (0,)), ((), ())), preferre...  54.4 us
    unnamed x5, waiting for transfers between devices  45.5 us
    all_gather x1, waiting for transfers between devices, body(): lax.all_gather(full_term.astype(jnp.bfloat16), 'gz')  43.3 us
    slice x32, local copies, waits for them, and re-layouts, conv_forward(): padded[shift_z:shift_z + size_z, shift_x:shift_x + size_x, shift_y:shift_...  41.4 us
    reshape x27, local copies, waits for them, and re-layouts, conv_forward(): window = window.reshape(count_cells, padded.shape[3])  40.1 us
    ppermute x7, starting transfers between devices, with_halo(): lax.ppermute(tail, axis, [(i, (i + 1) % count) for i in range(ends)])  28.8 us
    reduce_scatter x1, waiting for transfers between devices, body(): lax.psum_scatter(lift_features(bottle, own_up).astype(jnp.bfloat16), 'gz'...  26.3 us
  transfers between devices with their start and end apart: 19, of which 10 were waited for; matrix products, arithmetic and copies ran while one was open for 9% of the time, Pallas kernels for 0%

profile of v1, /device:TPU:0, one launch (start us, length us, event | category | flops | bytes accessed | tf_op | source)
XLA Modules:
  0.0 859.5 jit_solution(17248519154055112022)
XLA Ops:
  8.8 7.3 collective-permute-start
  18.6 7.1 collective-permute-done.1
  29.4 2.6 collective-permute-done.3
  32.0 2.9 collective-permute-start.4
  37.9 3.1 collective-permute-done.5
  47.4 14.3 %all_gather.7 = bf16[16,4,4,512]{3,2,1,0:T(4,128)(2,1)S(1)} all-gather(bf16[4,4,4,512]{3,2,1,0:T(4,128)(2,1)S(1)} %fusion.33), channel_id=1, replica_groups=mesh['gx'=8,'gy'=8,'gz'=4] {'gz'}, dimensions={0}, use_global_device_ids=true | all-gather | bytes 327680 | tf_op jit(solution)/shard_map/all_gather | solution.py:129
  63.2 5.0 collective-permute-start.6
  69.2 2.9 copy.315
  72.1 4.6 reshape.906
  76.7 3.9 all-to-all-start
  84.8 6.8 collective-permute-done.7
  97.4 5.3 reshape.907
  102.7 3.2 copy.316
  113.1 2.7 fusion.124
  206.5 7.4 collective-permute-start.10
  215.2 2.7 convert_bitcast_fusion
  217.9 3.7 copy.332
  223.5 3.0 collective-permute-start.12
  227.9 4.3 collective-permute-done.13
  247.7 45.4 %all-reduce.7.cloned.1.call-done = bf16[16,4,4,512]{3,2,1,0:T(4,128)(2,1)} async-done(((bf16[16,4,4,512]{3,2,1,0:T(4,128)(2,1)}), bf16[16,4,4,512]{3,2,1,0:T(4,128)(2,1)}) %all-reduce.7.cloned.1.call-update) | async-done | bytes 262160
  295.0 26.3 %reduce-scatter.4.cloned.1.call-done = bf16[8,8,8,128]{3,2,1,0:T(8,128)(2,1)} async-done(((bf16[32,8,8,128]{3,2,1,0:T(8,128)(2,1)}), bf16[8,8,8,128]{3,2,1,0:T(8,128)(2,1)}) %reduce-scatter.4.cloned.1.call-update) | async-done | bytes 131088 | tf_op jit(solution)/shard_map/reduce_scatter | solution.py:138
  375.9 43.3 %all-gather.2.cloned.1.call-done = bf16[4,128,27,128]{3,1,2,0:T(8,128)(2,1)} async-done(((bf16[1,128,27,128]{3,1,2,0:T(8,128)(2,1)}), bf16[4,128,27,128]{3,1,2,0:T(8,128)(2,1)}) %all-gather.2.cloned.1.call-update) | async-done | bytes 3538960 | tf_op jit(solution)/shard_map/all_gather | solution.py:165
  419.2 2.7 reduce_sum.12
  421.9 428.7 %all-reduce.8 = f32[128,27,128]{2,0,1:T(8,128)} all-reduce(bf16[128,27,128]{2,0,1:T(8,128)(2,1)S(1)} %reduce_sum.12), channel_id=4, replica_groups=mesh['gx'=8,'gy'=8,'gz'=4] {'gx','gy'}, use_global_device_ids=true, to_apply=%region_3.4.clone | all-reduce | flops 442368 | bytes 2654208
  (405 shorter events, 201.7 us)
Async XLA Ops:
  8.0 60.1 %copy-start = (bf16[8,512,128]{2,1,0:T(8,128)(2,1)S(1)}, bf16[8,512,128]{2,1,0:T(8,128)(2,1)}, u32[]{:S(2)}) copy-start(bf16[8,512,128]{2,1,0:T(8,128)(2,1)} %param.11) | copy-start | bytes 3145732
  8.8 8.8 %collective-permute-start = (bf16[8,1,8,128]{3,2,1,0:T(8,128)(2,1)S(1)}, bf16[8,1,8,128]{3,2,1,0:T(8,128)(2,1)S(1)}, u32[]{:S(2)}, u32[]{:S(2)}) collective-permute-start(bf16[8,1,8,128]{3,2,1,0:T(8,128)(2,1)S(1)} %get-tuple-element.94), channel_id=1, source_target_pairs={{0,32},{32,64},{64,96},{96,128},{128,160},{160,192},{192,224},{1,3... | collective-permute-start | bytes 49160 | tf_op jit(solution)/shard_map/ppermute | solution.py:15
  16.2 9.5 %collective-permute-start.1 = (bf16[8,1,8,128]{3,2,1,0:T(8,128)(2,1)S(1)}, bf16[8,1,8,128]{3,2,1,0:T(8,128)(2,1)S(1)}, u32[]{:S(2)}, u32[]{:S(2)}) collective-permute-start(bf16[8,1,8,128]{3,2,1,0:T(8,128)(2,1)S(1)} %get-tuple-element.93), channel_id=1, source_target_pairs={{32,0},{64,32},{96,64},{128,96},{160,128},{192,160},{224,192},{33,... | collective-permute-start | bytes 49160 | tf_op jit(solution)/shard_map/ppermute | solution.py:17
  18.6 18.2 %copy-start.53 = (bf16[8,9,8,128]{3,2,1,0:T(8,128)(2,1)}, bf16[8,9,8,128]{3,2,1,0:T(8,128)(2,1)S(1)}, u32[]{:S(2)}) copy-start(bf16[8,9,8,128]{3,2,1,0:T(8,128)(2,1)S(1)} %get-tuple-element.90) | copy-start | bytes 442372
  25.8 3.6 collective-permute-start.2
  27.1 4.8 collective-permute-start.3
  32.0 5.8 collective-permute-start.4
  35.0 6.0 collective-permute-start.5
  47.1 21.0 %copy-start.55 = (bf16[8,8,8,128]{3,2,1,0:T(8,128)(2,1)S(1)}, bf16[8,8,8,128]{3,2,1,0:T(8,128)(2,1)}, u32[]{:S(2)}) copy-start(bf16[8,8,8,128]{3,2,1,0:T(8,128)(2,1)} %param.7) | copy-start | bytes 393220
  63.2 19.7 %collective-permute-start.6 = (bf16[16,1,4,512]{3,0,2,1:T(8,128)(2,1)}, bf16[16,1,4,512]{3,0,2,1:T(8,128)(2,1)}, u32[]{:S(2)}, u32[]{:S(2)}) collective-permute-start(bf16[16,1,4,512]{3,0,2,1:T(8,128)(2,1)} %copy.428), channel_id=1, source_target_pairs={{0,32},{32,64},{64,96},{96,128},{128,160},{160,192},{192,224},{1,3... | collective-permute-start | bytes 196616 | tf_op jit(solution)/shard_map/ppermute | solution.py:15
  76.7 20.7 %all-to-all-start = ((bf16[4,2,4096]{2,1,0:T(2,128)(2,1)}), bf16[4,2,4096]{2,1,0:T(2,128)(2,1)}, u32[]{:S(2)}, u32[]{:S(2)}) async-start(bf16[4,2,4096]{2,1,0:T(2,128)(2,1)} %reshape.906), calls=%async_computation.1 | async-start | bytes 131072 | tf_op jit(solution)/shard_map/all_to_all | solution.py:143
  80.6 212.5 %all-reduce.7.cloned.1.call-start = ((), (), s32[]{:S(2)}) async-start(), calls=%async_computation.6 | async-start | bytes 524288
  81.5 10.1 %collective-permute-start.7 = (bf16[16,1,4,512]{3,0,2,1:T(8,128)(2,1)S(1)}, bf16[16,1,4,512]{3,0,2,1:T(8,128)(2,1)S(1)}, u32[]{:S(2)}, u32[]{:S(2)}) collective-permute-start(bf16[16,1,4,512]{3,0,2,1:T(8,128)(2,1)S(1)} %copy.429), channel_id=1, source_target_pairs={{32,0},{64,32},{96,64},{128,96},{160,128},{192,160},{224,192},{33,... | collective-permute-start | bytes 196616 | tf_op jit(solution)/shard_map/ppermute | solution.py:17
  92.4 20.7 %collective-permute-start.8 = (bf16[16,6,1,512]{3,0,2,1:T(8,128)(2,1)}, bf16[16,6,1,512]{3,0,2,1:T(8,128)(2,1)}, u32[]{:S(2)}, u32[]{:S(2)}) collective-permute-start(bf16[16,6,1,512]{3,0,2,1:T(8,128)(2,1)} %get-tuple-element.30), channel_id=1, source_target_pairs={{0,4},{4,8},{8,12},{12,16},{16,20},{20,24},{24,28},{1,5},{5,9},{9,... | collective-permute-start | bytes 294920 | tf_op jit(solution)/shard_map/ppermute | solution.py:15
  94.3 18.8 %collective-permute-start.9 = (bf16[16,6,1,512]{3,0,2,1:T(8,128)(2,1)}, bf16[16,6,1,512]{3,0,2,1:T(8,128)(2,1)}, u32[]{:S(2)}, u32[]{:S(2)}) collective-permute-start(bf16[16,6,1,512]{3,0,2,1:T(8,128)(2,1)} %get-tuple-element.31), channel_id=1, source_target_pairs={{4,0},{8,4},{12,8},{16,12},{20,16},{24,20},{28,24},{5,1},{9,5},{13... | collective-permute-start | bytes 294920 | tf_op jit(solution)/shard_map/ppermute | solution.py:17
  102.7 13.2 %copy-start.1 = (bf16[512,4,4,4]{3,2,1,0:T(4,128)(2,1)}, bf16[512,4,4,4]{3,2,1,0:T(4,128)(2,1)S(1)}, u32[]{:S(2)}) copy-start(bf16[512,4,4,4]{3,2,1,0:T(4,128)(2,1)S(1)} %reshape.907) | copy-start | bytes 196612
  206.5 15.1 %collective-permute-start.10 = (bf16[16,1,4,128]{3,0,2,1:T(8,128)(2,1)S(1)}, bf16[16,1,4,128]{3,0,2,1:T(8,128)(2,1)S(1)}, u32[]{:S(2)}, u32[]{:S(2)}) collective-permute-start(bf16[16,1,4,128]{3,0,2,1:T(8,128)(2,1)S(1)} %get-tuple-element.107), channel_id=1, source_target_pairs={{0,32},{32,64},{64,96},{96,128},{128,160},{160,192},{192,224},{1,3... | collective-permute-start | bytes 49160 | tf_op jit(solution)/shard_map/ppermute | solution.py:15
  213.9 9.5 %collective-permute-start.11 = (bf16[16,1,4,128]{3,0,2,1:T(8,128)(2,1)S(1)}, bf16[16,1,4,128]{3,0,2,1:T(8,128)(2,1)S(1)}, u32[]{:S(2)}, u32[]{:S(2)}) collective-permute-start(bf16[16,1,4,128]{3,0,2,1:T(8,128)(2,1)S(1)} %get-tuple-element.108), channel_id=1, source_target_pairs={{32,0},{64,32},{96,64},{128,96},{160,128},{192,160},{224,192},{33,... | collective-permute-start | bytes 49160 | tf_op jit(solution)/shard_map/ppermute | solution.py:17
  223.5 4.5 collective-permute-start.12
  226.5 5.8 collective-permute-start.13
  240.7 80.6 %reduce-scatter.4.cloned.1.call-start = ((), (), s32[]{:S(2)}) async-start(), calls=%async_computation.3 | async-start | bytes 655360 | tf_op jit(solution)/shard_map/reduce_scatter | solution.py:138
  243.8 175.4 %all-gather.2.cloned.1.call-start = ((), (), s32[]{:S(2)}) async-start(), calls=%async_computation.4 | async-start | bytes 4423680 | tf_op jit(solution)/shard_map/all_gather | solution.py:165
  245.8 77.4 %copy-start.6 = (bf16[9,10,10,128]{3,2,1,0:T(8,128)(2,1)S(1)}, bf16[9,10,10,128]{3,2,1,0:T(8,128)(2,1)}, u32[]{:S(2)}) copy-start(bf16[9,10,10,128]{3,2,1,0:T(8,128)(2,1)} %copy-done.5) | copy-start | bytes 691204
  345.9 506.3 %reduce-scatter.6.cloned.1.call-start = ((), (), s32[]{:S(2)}) async-start(), calls=%async_computation.5 | async-start | bytes 7188480 | tf_op jit(solution)/shard_map/reduce_scatter | solution.py:145
  (55 other events, 316.8 us)
Sparse Core Ops, SparseCore 0:
  240.8 52.2 all-reduce.6
  295.8 25.4 reduce-scatter.3
  346.0 73.1 all-gather.1
Sparse Core Ops, SparseCore 1:
  374.1 450.0 reduce-scatter.5
